TPU v7x, 32 devices: a whole 2x2x4 slice. The times are simulated.
32 devices in a mesh: groups: 2 (over y), seq: 4 (over z), tensor: 4 (over x, core).
Axes of the slice: x: 2, y: 2, z: 4, core: 2. Of those that a mesh axis runs over, the one named last changes fastest.
Arguments:
- video_query: bfloat16 [1024, 4096], P(('groups', 'seq'), 'tensor'), parts along dimension 0, may hold values from -21 to 21
- video_key: bfloat16 [1024, 4096], P(('groups', 'seq'), 'tensor'), parts along dimension 0, may hold values from -21 to 21
- video_value: bfloat16 [1024, 4096], P(('groups', 'seq'), 'tensor'), parts along dimension 0, may hold values from -6 to 6
- video_stream: bfloat16 [1024, 4096], P(('groups', 'seq'), 'tensor'), parts along dimension 0, may hold values from -6 to 6
- out_weight: bfloat16 [4096, 4096], P('tensor'), may hold values from -0.09375 to 0.09375
- cross_query: bfloat16 [1024, 2048], P(('groups', 'seq'), 'tensor'), parts along dimension 0, may hold values from -21 to 21
- audio_key: bfloat16 [128, 2048], P(('groups', 'seq'), 'tensor'), parts along dimension 0, may hold values from -21 to 21
- audio_value: bfloat16 [128, 2048], P(('groups', 'seq'), 'tensor'), parts along dimension 0, may hold values from -6 to 6
- audio_query: bfloat16 [128, 2048], P(('groups', 'seq'), 'tensor'), parts along dimension 0, may hold values from -21 to 21
- cross_key: bfloat16 [1024, 2048], P(('groups', 'seq'), 'tensor'), parts along dimension 0, may hold values from -21 to 21
- cross_value: bfloat16 [1024, 2048], P(('groups', 'seq'), 'tensor'), parts along dimension 0, may hold values from -6 to 6
Outputs:
- video_next: bfloat16 [1024, 4096], P(('groups', 'seq'), 'tensor'), parts along dimension 0
- video_cross: bfloat16 [1024, 2048], P(('groups', 'seq'), 'tensor'), parts along dimension 0
- audio_cross: bfloat16 [128, 2048], P(('groups', 'seq'), 'tensor'), parts along dimension 0
There are 2 independent parts, one for each index of `groups`. A program takes and returns all parts, laid end to end along the dimension named above; an argument that names none is the same for every part. Nothing has to cross between parts.
All inputs are finite; a program needn't handle non-finite values.
Results may differ from a plain program's by a relative error of at most 0.012.
Values may be sent and summed in bfloat16 or wider, within the bound.
A program may use at most 64 MiB of HBM per device.

v0:
```python
import math

import jax
import jax.numpy as jnp
from jax import lax
from jax.sharding import PartitionSpec as P

HD = 128


def blank_state(query_rows, head_count):
    return (
        jnp.full((head_count, query_rows), -1e30, jnp.float32),
        jnp.zeros((head_count, query_rows), jnp.float32),
        jnp.zeros((head_count, query_rows, HD), jnp.float32),
    )


def absorb(carried, queries, keyset, values, head_count):
    running, row_sum, numerator = carried
    query_rows = queries.shape[0]
    key_rows = keyset.shape[0]
    factor = 1.0 / math.sqrt(HD)
    query_heads = queries.reshape(query_rows, head_count, HD)
    for offset in range(0, key_rows, 1024):
        width_keys = min(1024, key_rows - offset)
        key_block = keyset[offset : offset + width_keys].reshape(width_keys, head_count, HD)
        value_block = values[offset : offset + width_keys].reshape(width_keys, head_count, HD)
        scores = (
            jnp.einsum("qhd,khd->hqk", query_heads, key_block, preferred_element_type=jnp.float32)
            * factor
        )
        highest = jnp.maximum(running, jnp.max(scores, axis=2))
        raised = jnp.exp(scores - highest[:, :, None])
        shrink = jnp.exp(running - highest)
        row_sum = row_sum * shrink + jnp.sum(raised, axis=2)
        numerator = numerator * shrink[:, :, None] + jnp.einsum(
            "hqk,khd->hqd",
            raised.astype(jnp.bfloat16),
            value_block,
            preferred_element_type=jnp.float32,
        )
        running = highest
    return (running, row_sum, numerator)


def finish(carried, head_count):
    running, row_sum, numerator = carried
    result = numerator / row_sum[:, :, None]
    return result.transpose(1, 0, 2).reshape(result.shape[1], head_count * HD).astype(jnp.bfloat16)


def local(
    video_query,
    video_key,
    video_value,
    video_stream,
    out_weight,
    cross_query,
    audio_key,
    audio_value,
    audio_query,
    cross_key,
    cross_value,
):
    local_heads = video_query.shape[1] // HD
    query_rows = video_query.shape[0]
    pieces = (
        lax.all_gather(video_key, "seq", axis=0, tiled=True),
        lax.all_gather(video_value, "seq", axis=0, tiled=True),
    )
    carried_video = absorb(
        blank_state(query_rows, local_heads), video_query, pieces[0], pieces[1], local_heads
    )
    attended = finish(carried_video, local_heads)
    projected = jnp.dot(attended, out_weight, preferred_element_type=jnp.float32)
    summed = lax.psum_scatter(
        projected.astype(jnp.bfloat16), "tensor", scatter_dimension=1, tiled=True
    ).astype(jnp.float32)
    video_next = (video_stream.astype(jnp.float32) + summed).astype(jnp.bfloat16)
    cross_heads = cross_query.shape[1] // HD
    every_key, every_value = (
        lax.all_gather(audio_key, "seq", axis=0, tiled=True),
        lax.all_gather(audio_value, "seq", axis=0, tiled=True),
    )
    carried_audio = absorb(
        blank_state(cross_query.shape[0], cross_heads),
        cross_query,
        every_key,
        every_value,
        cross_heads,
    )
    video_cross = finish(carried_audio, cross_heads)
    pieces = (
        lax.all_gather(cross_key, "seq", axis=0, tiled=True),
        lax.all_gather(cross_value, "seq", axis=0, tiled=True),
    )
    carried_cross = absorb(
        blank_state(audio_query.shape[0], cross_heads),
        audio_query,
        pieces[0],
        pieces[1],
        cross_heads,
    )
    audio_cross = finish(carried_cross, cross_heads)
    return (video_next, video_cross, audio_cross)


def solution(mesh):
    in_specs = (
        P(("groups", "seq"), "tensor"),
        P(("groups", "seq"), "tensor"),
        P(("groups", "seq"), "tensor"),
        P(("groups", "seq"), "tensor"),
        P("tensor", None),
        P(("groups", "seq"), "tensor"),
        P(("groups", "seq"), "tensor"),
        P(("groups", "seq"), "tensor"),
        P(("groups", "seq"), "tensor"),
        P(("groups", "seq"), "tensor"),
        P(("groups", "seq"), "tensor"),
    )
    out_specs = (
        P(("groups", "seq"), "tensor"),
        P(("groups", "seq"), "tensor"),
        P(("groups", "seq"), "tensor"),
    )
    return jax.shard_map(local, mesh=mesh, in_specs=in_specs, out_specs=out_specs, check_vma=False)
```

profile of v0, /device:TPU:0, one launch (start us, length us, event | category | flops | bytes accessed | tf_op | source)
XLA Modules:
  0.0 119.0 jit_solution(1426176765482469748)
XLA Ops:
  7.2 1.8 %copy.19 = bf16[128,1024]{0,1:T(8,128)(2,1)} copy(bf16[128,1024]{1,0:T(8,128)(2,1)} %param.12) | data formatting | bytes 524288 | tf_op args[1]
  9.1 0.0 all-gather.5.cloned.1.call-start
  9.1 0.7 all-gather.5.cloned.1.call-update
  9.9 15.2 %all_gather.20 = bf16[64,512]{1,0:T(8,128)(2,1)S(1)} all-gather(bf16[16,512]{1,0:T(8,128)(2,1)} %param.17), channel_id=1, replica_groups=mesh['groups'=2,'seq'=4,'tensor'=4] {'seq'}, dimensions={0}, use_global_device_ids=true | all-gather | bytes 81920 | tf_op jit(solution)/shard_map/all_gather | solution.py:83
  25.1 16.4 %all_gather.21 = bf16[64,512]{1,0:T(8,128)(2,1)} all-gather(bf16[16,512]{1,0:T(8,128)(2,1)} %param.18), channel_id=1, replica_groups=mesh['groups'=2,'seq'=4,'tensor'=4] {'seq'}, dimensions={0}, use_global_device_ids=true | all-gather | bytes 81920 | tf_op jit(solution)/shard_map/all_gather | solution.py:84
  41.5 1.1 fusion.35
  42.6 0.5 all-gather.3.cloned.1.call-done
  43.1 1.7 %multiply_reduce_fusion = (f32[8,128]{1,0:T(8,128)S(1)}, f32[8,128,512]{2,1,0:T(8,128)S(1)}) fusion(bf16[512,8,128]{0,2,1:T(8,128)(2,1)} %bitcast.107, bf16[128,1024]{1,0:T(8,128)(2,1)S(1)} %copy-done), kind=kOutput, calls=%fused_computation.2 | convolution fusion | flops 135265280 | bytes 3411968 | tf_op jit(solution)/shard_map/qhd,khd->hqk/dot_general | solution.py:30
  44.8 0.6 fusion
  45.4 26.0 %all-gather.5.cloned.1.call-done = bf16[512,1024]{1,0:T(8,128)(2,1)} async-done(((bf16[128,1024]{1,0:T(8,128)(2,1)}), bf16[512,1024]{1,0:T(8,128)(2,1)}) %all-gather.5.cloned.1.call-update) | async-done | bytes 1048592 | tf_op jit(solution)/shard_map/all_gather | solution.py:70
  71.4 1.5 %copy.22 = bf16[512,1024]{0,1:T(8,128)(2,1)S(1)} copy(bf16[512,1024]{1,0:T(8,128)(2,1)} %all-gather.5.cloned.1.call-done) | data formatting | bytes 2097152 | tf_op jit(solution)/shard_map/all_gather | solution.py:70
  72.9 0.6 fusion.4
  73.5 5.7 %convolution_convert_fusion = bf16[128,4096]{1,0:T(8,128)(2,1)} fusion(bf16[128,1024]{0,1:T(8,128)(2,1)S(1)} %bitcast.108, bf16[1024,4096]{1,0:T(8,128)(2,1)} %param.15), kind=kOutput, calls=%fused_computation | convolution fusion | flops 1074266112 | bytes 9699328 | tf_op jit(solution)/shard_map/dot_general | solution.py:76
  79.3 0.2 fusion.7
  79.6 0.8 copy.32
  80.3 0.1 copy.29
  80.5 0.1 copy.26
  80.6 14.9 %all_gather.22 = bf16[512,512]{0,1:T(8,128)(2,1)S(1)} all-gather(bf16[128,512]{0,1:T(8,128)(2,1)S(1)} %copy.26), channel_id=1, replica_groups=mesh['groups'=2,'seq'=4,'tensor'=4] {'seq'}, dimensions={0}, use_global_device_ids=true | all-gather | bytes 655360 | tf_op jit(solution)/shard_map/all_gather | solution.py:95
  95.5 0.3 fusion.36
  95.8 0.2 fusion.22
  96.0 13.9 %all_gather.23 = bf16[512,512]{0,1:T(8,128)(2,1)S(1)} all-gather(bf16[128,512]{0,1:T(8,128)(2,1)S(1)} %copy.29), channel_id=1, replica_groups=mesh['groups'=2,'seq'=4,'tensor'=4] {'seq'}, dimensions={0}, use_global_device_ids=true | all-gather | bytes 655360 | tf_op jit(solution)/shard_map/all_gather | solution.py:96
  109.9 0.3 fusion.11
  110.2 0.6 copy.71
  110.8 1.7 %add_convert_fusion = bf16[128,1024]{1,0:T(8,128)(2,1)} fusion(bf16[128,1024]{1,0:T(8,128)(2,1)} %reduce-scatter.2.cloned.1.call-done, bf16[128,1024]{1,0:T(8,128)(2,1)S(1)} %copy-done.1), kind=kLoop, calls=%fused_computation.22 | loop fusion | flops 524288 | bytes 786432 | tf_op jit(solution)/shard_map/convert_element_type | solution.py:80
  (24 shorter events, 0.2 us)
Async XLA Ops:
  7.2 35.9 %copy-start = (bf16[128,1024]{1,0:T(8,128)(2,1)S(1)}, bf16[128,1024]{1,0:T(8,128)(2,1)}, u32[]{:S(2)}) copy-start(bf16[128,1024]{1,0:T(8,128)(2,1)} %param.11) | copy-start | bytes 786436
  7.2 35.9 %all-gather.3.cloned.1.call-start = ((), (), s32[]{:S(2)}) async-start(), calls=%async_computation.1 | async-start | bytes 1310720 | tf_op jit(solution)/shard_map/all_gather | solution.py:69
  9.1 62.3 %all-gather.5.cloned.1.call-start = ((), (), s32[]{:S(2)}) async-start(), calls=%async_computation.2 | async-start | bytes 1310720 | tf_op jit(solution)/shard_map/all_gather | solution.py:70
  9.8 101.0 %reduce-scatter.2.cloned.1.call-start = ((), (), s32[]{:S(2)}) async-start(), calls=%async_computation.3 | async-start | bytes 1310720 | tf_op jit(solution)/shard_map/reduce_scatter | solution.py:77
  73.5 5.8 %copy-start.4 = (bf16[64,512]{1,0:T(8,128)(2,1)S(1)}, bf16[64,512]{1,0:T(8,128)(2,1)}, u32[]{:S(2)}) copy-start(bf16[64,512]{1,0:T(8,128)(2,1)} %all_gather.21) | copy-start | bytes 196612
  79.2 1.1 copy-start.2
  79.2 1.3 %copy-start.3 = (bf16[128,512]{1,0:T(8,128)(2,1)S(1)}, bf16[128,512]{1,0:T(8,128)(2,1)}, u32[]{:S(2)}) copy-start(bf16[128,512]{1,0:T(8,128)(2,1)} %param.20) | copy-start | bytes 393220
  79.2 16.3 %copy-start.5 = (bf16[16,512]{1,0:T(8,128)(2,1)S(1)}, bf16[16,512]{1,0:T(8,128)(2,1)}, u32[]{:S(2)}) copy-start(bf16[16,512]{1,0:T(8,128)(2,1)} %param.19) | copy-start | bytes 49156
  79.6 31.2 %copy-start.1 = (bf16[128,1024]{1,0:T(8,128)(2,1)S(1)}, bf16[128,1024]{1,0:T(8,128)(2,1)}, u32[]{:S(2)}) copy-start(bf16[128,1024]{1,0:T(8,128)(2,1)} %param.14) | copy-start | bytes 786436
Sparse Core Ops, SparseCore 0:
  10.1 32.9 all-gather.2
  44.6 26.7 all-gather.4
  79.3 24.1 reduce-scatter.1
where the time goes:
time: 119 us
  blocking collectives  60.4 us (51%)
  waiting for transfers between devices  27.2 us (23%)
  between operations  13.9 us (12%)
  matrix products  9.91 us (8%)
  local copies, waits for them, and re-layouts  4.99 us (4%)
  other arithmetic  2.58 us (2%)
    all_gather x1, waiting for transfers between devices, local(): lax.all_gather(video_value, 'seq', axis=0, tiled=True)  26 us
    all_gather x1, blocking collectives, local(): lax.all_gather(audio_value, 'seq', axis=0, tiled=True)  16.4 us
    all_gather x1, blocking collectives, local(): lax.all_gather(audio_key, 'seq', axis=0, tiled=True)  15.2 us
    all_gather x1, blocking collectives, local(): lax.all_gather(cross_key, 'seq', axis=0, tiled=True)  14.9 us
    all_gather x1, blocking collectives, local(): lax.all_gather(cross_value, 'seq', axis=0, tiled=True)  13.9 us
    dot_general x1, matrix products, local(): jnp.dot(attended, out_weight, preferred_element_type=jnp.float32)  5.7 us
    dot_general x3, matrix products, absorb(): jnp.einsum('qhd,khd->hqk', query_heads, key_block, preferred_element_type...  3.1 us
    unnamed x16, local copies, waits for them, and re-layouts  2.86 us
  transfers between devices with their start and end apart: 3, of which 2 were waited for; matrix products, arithmetic and copies ran while one was open for 5% of the time, Pallas kernels for 0%

commit v1 on v0

--- a/solution.py
+++ b/solution.py
@@ -1,8 +1,11 @@
+import functools
 import math
 
 import jax
 import jax.numpy as jnp
 from jax import lax
+from jax.experimental import pallas as pl
+from jax.experimental.pallas import tpu as pltpu
 from jax.sharding import PartitionSpec as P
 
 HD = 128
@@ -106,7 +109,452 @@
     return (video_next, video_cross, audio_cross)
 
 
+MESH = pl.DeviceIdType.MESH
+NT = (((1,), (1,)), ((), ()))
+WIDE = 256
+
+
+def softmax_parts(queries, keyset, values):
+    scores = lax.dot_general(queries, keyset, NT, preferred_element_type=jnp.float32) * (
+        1.0 / math.sqrt(HD)
+    )
+    highest = jnp.max(scores, axis=1, keepdims=True)
+    raised = jnp.exp(scores - highest)
+    row_sum = jnp.sum(raised, axis=1, keepdims=True)
+    numerator = jnp.dot(raised.astype(jnp.bfloat16), values, preferred_element_type=jnp.float32)
+    return highest, row_sum, numerator
+
+
+def block_kernel(
+    seq,
+    tensor,
+    vq,
+    vk,
+    vv,
+    vs,
+    weight,
+    cq,
+    ak,
+    av,
+    aq,
+    ck,
+    cv,
+    next_ref,
+    vcross_ref,
+    across_ref,
+    qkv,
+    heads_out,
+    gathered,
+    audio,
+    partial,
+    stats,
+    partial_in,
+    stats_in,
+    cq_v,
+    ck_v,
+    cv_v,
+    stream_v,
+    weight_v,
+    total,
+    pair_out,
+    pair_in,
+    far_out,
+    far_in,
+    qkv_send,
+    qkv_recv,
+    own_sem,
+    out_send,
+    out_recv,
+    audio_send,
+    audio_recv,
+    audio_own,
+    part_send,
+    part_recv,
+    stat_send,
+    stat_recv,
+    load_sem,
+    weight_sem,
+    pair_send,
+    pair_recv,
+    far_send,
+    far_recv,
+):
+    rows = vq.shape[0]
+    share = vq.shape[1] // HD // seq
+    cross_heads = cq.shape[1] // HD
+    audio_rows = aq.shape[0]
+    chips = tensor // 2
+    width = next_ref.shape[1]
+    pieces = width // WIDE
+    me = lax.axis_index("seq")
+    place = lax.axis_index("tensor")
+    core = lax.rem(place, 2)
+    chip = place // 2
+    sibling = chip * 2 + (1 - core)
+    peers = [lax.rem(me + d, seq) for d in range(1, seq)]
+    far_chips = [lax.rem(chip + d, chips) for d in range(chips)]
+
+    my_rows = pl.ds(pl.multiple_of(me * rows, rows), rows)
+    my_audio = pl.ds(pl.multiple_of(me * audio_rows, audio_rows), audio_rows)
+
+    def head_cols(owner, h):
+        return pl.ds(pl.multiple_of((owner * share + h) * HD, HD), HD)
+
+    local_copies = []
+    for h in range(share):
+        for kind, ref in enumerate((vk, vv, vq)):
+            copy = pltpu.make_async_copy(
+                ref.at[:, head_cols(me, h)], qkv.at[kind, h, my_rows], own_sem.at[kind, h]
+            )
+            copy.start()
+            local_copies.append(copy)
+    audio_copies = []
+    for kind, ref in enumerate((ak, av, aq)):
+        copy = pltpu.make_async_copy(ref, audio.at[kind, my_audio], audio_own.at[kind])
+        copy.start()
+        audio_copies.append(copy)
+    loads = []
+    for i, (ref, dst) in enumerate(((cq, cq_v), (ck, ck_v), (cv, cv_v), (vs, stream_v))):
+        copy = pltpu.make_async_copy(ref, dst, load_sem.at[i])
+        copy.start()
+        loads.append(copy)
+
+    barrier = pltpu.get_barrier_semaphore()
+    for p in peers:
+        pl.semaphore_signal(barrier, inc=1, device_id={"seq": p}, device_id_type=MESH)
+    pl.semaphore_signal(barrier, inc=1, device_id={"tensor": sibling}, device_id_type=MESH)
+    for d in range(1, chips):
+        pl.semaphore_signal(
+            barrier, inc=1, device_id={"tensor": far_chips[d] * 2 + core}, device_id_type=MESH
+        )
+    pl.semaphore_wait(barrier, seq - 1 + chips)
+
+    sends = []
+
+    def send_heads(h):
+        for kind, ref in enumerate((vk, vv, vq)):
+            for p in peers:
+                copy = pltpu.make_async_remote_copy(
+                    src_ref=ref.at[:, head_cols(p, h)],
+                    dst_ref=qkv.at[kind, h, my_rows],
+                    send_sem=qkv_send.at[kind, h, p],
+                    recv_sem=qkv_recv.at[kind, h, me],
+                    device_id={"seq": p},
+                    device_id_type=MESH,
+                )
+                copy.start()
+                sends.append(copy)
+
+    send_heads(0)
+    for kind, ref in enumerate((ak, av, aq)):
+        for p in peers:
+            copy = pltpu.make_async_remote_copy(
+                src_ref=ref,
+                dst_ref=audio.at[kind, my_audio],
+                send_sem=audio_send.at[kind, p],
+                recv_sem=audio_recv.at[kind, me],
+                device_id={"seq": p},
+                device_id_type=MESH,
+            )
+            copy.start()
+            sends.append(copy)
+    for h in range(1, share):
+        send_heads(h)
+
+    weight_copies = []
+    for h in range(share):
+        for p in range(seq):
+            copy = pltpu.make_async_copy(
+                weight.at[pl.ds((p * share + h) * HD, HD)],
+                weight_v.at[h, pl.ds(p * HD, HD)],
+                weight_sem.at[h, p],
+            )
+            copy.start()
+            weight_copies.append(copy)
+
+    def wait_from(src, dst, send_sem, recv_sem, p):
+        pltpu.make_async_remote_copy(
+            src_ref=src,
+            dst_ref=dst,
+            send_sem=send_sem,
+            recv_sem=recv_sem,
+            device_id={"seq": p},
+            device_id_type=MESH,
+        ).wait_recv()
+
+    def rows_of(p):
+        return pl.ds(pl.multiple_of(p * rows, rows), rows)
+
+    def audio_rows_of(p):
+        return pl.ds(pl.multiple_of(p * audio_rows, audio_rows), audio_rows)
+
+    def attend_head(h):
+        for kind in range(3):
+            local_copies[h * 3 + kind].wait()
+        for kind in range(3):
+            for p in peers:
+                wait_from(
+                    vk.at[:, head_cols(p, h)],
+                    qkv.at[kind, h, rows_of(p)],
+                    qkv_send.at[kind, h, p],
+                    qkv_recv.at[kind, h, p],
+                    p,
+                )
+        keyset, values = qkv[0, h], qkv[1, h]
+        for p in peers + [me]:
+            _, row_sum, numerator = softmax_parts(qkv[2, h, rows_of(p)], keyset, values)
+            result = (numerator / row_sum).astype(jnp.bfloat16)
+            if p is me:
+                gathered[h, me] = result
+            else:
+                heads_out[h, p] = result
+                copy = pltpu.make_async_remote_copy(
+                    src_ref=heads_out.at[h, p],
+                    dst_ref=gathered.at[h, me],
+                    send_sem=out_send.at[h, p],
+                    recv_sem=out_recv.at[h, me],
+                    device_id={"seq": p},
+                    device_id_type=MESH,
+                )
+                copy.start()
+                sends.append(copy)
+
+    def cross_parts():
+        for i in range(3):
+            loads[i].wait()
+        for kind in range(3):
+            audio_copies[kind].wait()
+            for p in peers:
+                wait_from(
+                    ak,
+                    audio.at[kind, audio_rows_of(p)],
+                    audio_send.at[kind, p],
+                    audio_recv.at[kind, p],
+                    p,
+                )
+        lane = lax.broadcasted_iota(jnp.int32, (seq * audio_rows, HD), 1)
+        held = jnp.zeros((seq * audio_rows, HD), jnp.float32)
+        for c in range(cross_heads):
+            cols = slice(c * HD, (c + 1) * HD)
+            highest, row_sum, numerator = softmax_parts(audio[2, :, cols], ck_v[:, cols], cv_v[:, cols])
+            held = jnp.where(lane == c, highest, held)
+            held = jnp.where(lane == cross_heads + c, row_sum, held)
+            partial[:, cols] = numerator.astype(jnp.bfloat16)
+        stats[...] = held
+        for p in peers:
+            for src, dst, s_sem, r_sem in (
+                (partial, partial_in, part_send, part_recv),
+                (stats, stats_in, stat_send, stat_recv),
+            ):
+                copy = pltpu.make_async_remote_copy(
+                    src_ref=src.at[audio_rows_of(p)],
+                    dst_ref=dst.at[me],
+                    send_sem=s_sem.at[p],
+                    recv_sem=r_sem.at[me],
+                    device_id={"seq": p},
+                    device_id_type=MESH,
+                )
+                copy.start()
+                sends.append(copy)
+        for c in range(cross_heads):
+            cols = slice(c * HD, (c + 1) * HD)
+            _, row_sum, numerator = softmax_parts(cq_v[:, cols], audio[0, :, cols], audio[1, :, cols])
+            vcross_ref[:, cols] = (numerator / row_sum).astype(jnp.bfloat16)
+
+    def cross_finish():
+        for p in peers:
+            wait_from(partial.at[audio_rows_of(p)], partial_in.at[p], part_send.at[p], part_recv.at[p], p)
+            wait_from(stats.at[audio_rows_of(p)], stats_in.at[p], stat_send.at[p], stat_recv.at[p], p)
+        held = [stats[my_audio, :]] + [stats_in[p] for p in peers]
+        for c in range(cross_heads):
+            cols = slice(c * HD, (c + 1) * HD)
+            parts = [partial[my_audio, cols]] + [partial_in[p, :, cols] for p in peers]
+            tops = [s[:, c : c + 1] for s in held]
+            sums = [s[:, cross_heads + c : cross_heads + c + 1] for s in held]
+            highest = functools.reduce(jnp.maximum, tops)
+            factors = [jnp.exp(t - highest) for t in tops]
+            row_sum = sum(f * s for f, s in zip(factors, sums))
+            numerator = sum(f * n.astype(jnp.float32) for f, n in zip(factors, parts))
+            across_ref[:, cols] = (numerator / row_sum).astype(jnp.bfloat16)
+
+    def wait_heads(h):
+        for p in peers:
+            wait_from(heads_out.at[h, p], gathered.at[h, p], out_send.at[h, p], out_recv.at[h, p], p)
+        for p in range(seq):
+            weight_copies[h * seq + p].wait()
+        return jnp.concatenate([gathered[h, p] for p in range(seq)], axis=1)
+
+    def product(attended, h, target, j):
+        cols = pl.ds(pl.multiple_of(target * width + j * WIDE, WIDE), WIDE)
+        return jnp.dot(attended, weight_v[h, :, cols], preferred_element_type=jnp.float32)
+
+    attend_head(0)
+    cross_parts()
+    for h in range(1, share):
+        attend_head(h)
+    cross_finish()
+    loads[3].wait()
+
+    slots = [(d, side) for d in list(range(1, chips)) + [0] for side in range(2)]
+
+    def owner_of(d, side):
+        return far_chips[d] * 2 + (core if side else 1 - core)
+
+    for h in range(share - 1):
+        attended = wait_heads(h)
+        for d, side in slots:
+            for j in range(pieces):
+                value = product(attended, h, owner_of(d, side), j)
+                if h:
+                    value = value + total[d, side, j]
+                total[d, side, j] = value
+    last = share - 1
+    attended = wait_heads(last)
+
+    def final(d, side, j):
+        value = product(attended, last, owner_of(d, side), j)
+        if last:
+            value = value + total[d, side, j]
+        return value
+
+    def pair_copy(d, j):
+        return pltpu.make_async_remote_copy(
+            src_ref=pair_out.at[d, j],
+            dst_ref=pair_in.at[d, j],
+            send_sem=pair_send.at[d, j],
+            recv_sem=pair_recv.at[d, j],
+            device_id={"tensor": sibling},
+            device_id_type=MESH,
+        )
+
+    def far_copy(d, j):
+        return pltpu.make_async_remote_copy(
+            src_ref=far_out.at[d - 1, j],
+            dst_ref=far_in.at[d - 1, j],
+            send_sem=far_send.at[d - 1, j],
+            recv_sem=far_recv.at[d - 1, j],
+            device_id={"tensor": far_chips[d] * 2 + core},
+            device_id_type=MESH,
+        )
+
+    def send_pair(d, j):
+        pair_out[d, j] = final(d, 0, j).astype(jnp.bfloat16)
+        copy = pair_copy(d, j)
+        copy.start()
+        sends.append(copy)
+
+    def send_far(d, j, value):
+        pair_copy(d, j).wait_recv()
+        far_out[d - 1, j] = (value + pair_in[d, j].astype(jnp.float32)).astype(jnp.bfloat16)
+        copy = far_copy(d, j)
+        copy.start()
+        sends.append(copy)
+
+    steps = [(d, j) for d in range(1, chips) for j in range(pieces)]
+    for d, j in steps:
+        send_pair(d, j)
+    for d, j in steps:
+        send_far(d, j, final(d, 1, j))
+    for j in range(pieces):
+        send_pair(0, j)
+    for j in range(pieces):
+        total[0, 1, j] = final(0, 1, j) + stream_v[:, j * WIDE : (j + 1) * WIDE].astype(jnp.float32)
+    for j in range(pieces):
+        pair_copy(0, j).wait_recv()
+        value = total[0, 1, j] + pair_in[0, j].astype(jnp.float32)
+        for d in range(1, chips):
+            far_copy(d, j).wait_recv()
+            value = value + far_in[d - 1, j].astype(jnp.float32)
+        next_ref[:, j * WIDE : (j + 1) * WIDE] = value.astype(jnp.bfloat16)
+    for copy in sends:
+        copy.wait_send()
+
+
+def fused(seq, tensor, *operands):
+    vq, vk, vv, vs, weight, cq, ak, av, aq, ck, cv = operands
+    rows, features = vq.shape
+    share = features // HD // seq
+    audio_rows, cross_width = aq.shape
+    chips = tensor // 2
+    width = weight.shape[1] // tensor
+    pieces = width // WIDE
+    bf16, f32, dma = jnp.bfloat16, jnp.float32, pltpu.SemaphoreType.DMA
+    return pl.pallas_call(
+        functools.partial(block_kernel, seq, tensor),
+        out_shape=(
+            jax.ShapeDtypeStruct(vs.shape, bf16),
+            jax.ShapeDtypeStruct(cq.shape, bf16),
+            jax.ShapeDtypeStruct(aq.shape, bf16),
+        ),
+        in_specs=[pl.BlockSpec(memory_space=pl.ANY)] * 11,
+        out_specs=tuple([pl.BlockSpec(memory_space=pltpu.VMEM)] * 3),
+        scratch_shapes=[
+            pltpu.VMEM((3, share, seq * rows, HD), bf16),
+            pltpu.VMEM((share, seq, rows, HD), bf16),
+            pltpu.VMEM((share, seq, rows, HD), bf16),
+            pltpu.VMEM((3, seq * audio_rows, cross_width), bf16),
+            pltpu.VMEM((seq * audio_rows, cross_width), bf16),
+            pltpu.VMEM((seq * audio_rows, HD), f32),
+            pltpu.VMEM((seq, audio_rows, cross_width), bf16),
+            pltpu.VMEM((seq, audio_rows, HD), f32),
+            pltpu.VMEM(cq.shape, bf16),
+            pltpu.VMEM(ck.shape, bf16),
+            pltpu.VMEM(cv.shape, bf16),
+            pltpu.VMEM(vs.shape, bf16),
+            pltpu.VMEM((share, seq * HD, weight.shape[1]), bf16),
+            pltpu.VMEM((chips, 2, pieces, rows, WIDE), f32),
+            pltpu.VMEM((chips, pieces, rows, WIDE), bf16),
+            pltpu.VMEM((chips, pieces, rows, WIDE), bf16),
+            pltpu.VMEM((max(chips - 1, 1), pieces, rows, WIDE), bf16),
+            pltpu.VMEM((max(chips - 1, 1), pieces, rows, WIDE), bf16),
+            dma((3, share, seq)),
+            dma((3, share, seq)),
+            dma((3, share)),
+            dma((share, seq)),
+            dma((share, seq)),
+            dma((3, seq)),
+            dma((3, seq)),
+            dma((3,)),
+            dma((seq,)),
+            dma((seq,)),
+            dma((seq,)),
+            dma((seq,)),
+            dma((4,)),
+            dma((share, seq)),
+            dma((chips, pieces)),
+            dma((chips, pieces)),
+            dma((max(chips - 1, 1), pieces)),
+            dma((max(chips - 1, 1), pieces)),
+        ],
+        compiler_params=pltpu.CompilerParams(
+            collective_id=0, has_side_effects=True, vmem_limit_bytes=60000000
+        ),
+    )(*operands)
+
+
+def fits(mesh, operands):
+    seq, tensor = mesh.shape["seq"], mesh.shape["tensor"]
+    vq, weight, cq, aq = operands[0], operands[4], operands[5], operands[8]
+    return (
+        seq > 1
+        and (vq.shape[1] // HD) % seq == 0
+        and tensor % 2 == 0
+        and (weight.shape[1] // tensor) % WIDE == 0
+        and aq.shape[0] % 16 == 0
+        and vq.shape[0] % 16 == 0
+        and 2 * (cq.shape[1] // HD) <= HD
+        and weight.size * 2 <= 16 * 2**20
+        and vq.shape[0] <= 256
+        and seq <= 8
+    )
+
+
 def solution(mesh):
+    def step(*operands):
+        if fits(mesh, operands):
+            return fused(mesh.shape["seq"], mesh.shape["tensor"], *operands)
+        return local(*operands)
+
     in_specs = (
         P(("groups", "seq"), "tensor"),
         P(("groups", "seq"), "tensor"),
@@ -125,4 +573,4 @@
         P(("groups", "seq"), "tensor"),
         P(("groups", "seq"), "tensor"),
     )
-    return jax.shard_map(local, mesh=mesh, in_specs=in_specs, out_specs=out_specs, check_vma=False)
+    return jax.shard_map(step, mesh=mesh, in_specs=in_specs, out_specs=out_specs, check_vma=False)

time: 119 us -> 52.8 us (0.44)
  blocking collectives: 60.4 us -> 0 us
  Pallas kernels: 0 us -> 47.3 us
  waiting for transfers between devices: 27.2 us -> 0 us
  between operations: 13.9 us -> 0.64 us
  matrix products: 9.91 us -> 0 us
  other arithmetic: 2.58 us -> 0 us
    all_gather x4 -> x0, blocking collectives: 60.4 us -> none  [the longest x1 16.4 us: local(): lax.all_gather(audio_value, 'seq', axis=0, tiled=True)]
    pallas_call x0 -> x1, Pallas kernels: none -> 47.3 us  [fused(): pl.pallas_call(functools.partial(block_kernel, seq, tensor), out_shape=(j...]
    all_gather x2 -> x0, waiting for transfers between devices: 26.5 us -> none  [the longest x1 26 us: local(): lax.all_gather(video_value, 'seq', axis=0, tiled=True)]
    dot_general x7 -> x0, matrix products: 9.91 us -> none  [the longest x1 5.7 us: local(): jnp.dot(attended, out_weight, preferred_element_type=jnp.float32)]
    convert_element_type x1 -> x0, other arithmetic: 1.72 us -> none  [local(): (video_stream.astype(jnp.float32) + summed).astype(jnp.bfloat16)]
    unnamed x16 -> x3, local copies, waits for them, and re-layouts: 2.86 us -> 4.56 us
    all_gather x1 -> x0, local copies, waits for them, and re-layouts: 1.49 us -> none  [local(): lax.all_gather(video_value, 'seq', axis=0, tiled=True)]
  transfers between devices with their start and end apart: 3 -> 0, of which waited for: 2 -> 0; matrix products, arithmetic and copies ran while one was open for 5% -> 0% of each run, Pallas kernels for 0% -> 0%
where the time goes in v1:
time: 52.8 us; the launch traced here: 52.5 us
  Pallas kernels  47.3 us (90%)
  local copies, waits for them, and re-layouts  4.56 us (9%)
  between operations  0.64 us (1%)
    pallas_call x1, Pallas kernels, fused(): pl.pallas_call(functools.partial(block_kernel, seq, tensor), out_shape=(j...  47.3 us
    unnamed x3, local copies, waits for them, and re-layouts  4.56 us

profile of v1, /device:TPU:0, one launch (start us, length us, event | category | flops | bytes accessed | tf_op | source)
XLA Modules:
  0.0 52.5 jit_solution(6936714359961066389)
XLA Ops:
  0.6 47.3 %shard_map.130 = (bf16[128,1024]{1,0:T(8,128)(2,1)}, bf16[128,512]{1,0:T(8,128)(2,1)}, bf16[16,512]{1,0:T(8,128)(2,1)}) custom-call(bf16[128,1024]{1,0:T(8,128)(2,1)} %vq.1, bf16[128,1024]{1,0:T(8,128)(2,1)} %vk.1, bf16[128,1024]{1,0:T(8,128)(2,1)} %vv.1, bf16[128,1024]{1,0:T(8,128)(2,1)} %vs.1, bf16[1024,4096]{1,0:T(8,128)(2,1)} %weight.1, ...), custom_call_target="tpu_custom_call" | custom-call | tf_op jit(solution)/shard_map/pallas_call | solution.py:482
  47.9 1.7 %copy.17 = bf16[128,1024]{1,0:T(8,128)(2,1)} copy(bf16[128,1024]{1,0:T(8,128)(2,1)} %get-tuple-element.6) | data formatting | bytes 524288
  49.6 1.6 %copy.18 = bf16[128,512]{1,0:T(8,128)(2,1)} copy(bf16[128,512]{1,0:T(8,128)(2,1)} %get-tuple-element.7) | data formatting | bytes 262144
  51.2 1.3 %copy.19 = bf16[16,512]{1,0:T(8,128)(2,1)} copy(bf16[16,512]{1,0:T(8,128)(2,1)} %get-tuple-element.8) | data formatting | bytes 32768

commit v2 on v1

--- a/solution.py
+++ b/solution.py
@@ -112,6 +112,7 @@
 MESH = pl.DeviceIdType.MESH
 NT = (((1,), (1,)), ((), ()))
 WIDE = 256
+FIRST = 3
 
 
 def softmax_parts(queries, keyset, values):
@@ -155,13 +156,15 @@
     cv_v,
     stream_v,
     weight_v,
-    total,
+    kept,
     pair_out,
     pair_in,
     far_out,
     far_in,
-    qkv_send,
-    qkv_recv,
+    kv_send,
+    kv_recv,
+    q_send,
+    q_recv,
     own_sem,
     out_send,
     out_recv,
@@ -186,6 +189,7 @@
     chips = tensor // 2
     width = next_ref.shape[1]
     pieces = width // WIDE
+    cuts = row_cuts(rows)
     me = lax.axis_index("seq")
     place = lax.axis_index("tensor")
     core = lax.rem(place, 2)
@@ -231,56 +235,62 @@
 
     sends = []
 
-    def send_heads(h):
-        for kind, ref in enumerate((vk, vv, vq)):
-            for p in peers:
-                copy = pltpu.make_async_remote_copy(
-                    src_ref=ref.at[:, head_cols(p, h)],
-                    dst_ref=qkv.at[kind, h, my_rows],
-                    send_sem=qkv_send.at[kind, h, p],
-                    recv_sem=qkv_recv.at[kind, h, me],
-                    device_id={"seq": p},
-                    device_id_type=MESH,
-                )
-                copy.start()
-                sends.append(copy)
-
-    send_heads(0)
-    for kind, ref in enumerate((ak, av, aq)):
-        for p in peers:
-            copy = pltpu.make_async_remote_copy(
-                src_ref=ref,
-                dst_ref=audio.at[kind, my_audio],
-                send_sem=audio_send.at[kind, p],
-                recv_sem=audio_recv.at[kind, me],
-                device_id={"seq": p},
-                device_id_type=MESH,
-            )
-            copy.start()
-            sends.append(copy)
-    for h in range(1, share):
-        send_heads(h)
-
-    weight_copies = []
-    for h in range(share):
-        for p in range(seq):
-            copy = pltpu.make_async_copy(
-                weight.at[pl.ds((p * share + h) * HD, HD)],
-                weight_v.at[h, pl.ds(p * HD, HD)],
-                weight_sem.at[h, p],
-            )
-            copy.start()
-            weight_copies.append(copy)
-
-    def wait_from(src, dst, send_sem, recv_sem, p):
-        pltpu.make_async_remote_copy(
+    def to_seq(src, dst, send_sem, recv_sem, p):
+        return pltpu.make_async_remote_copy(
             src_ref=src,
             dst_ref=dst,
             send_sem=send_sem,
             recv_sem=recv_sem,
             device_id={"seq": p},
             device_id_type=MESH,
-        ).wait_recv()
+        )
+
+    def launch(copy):
+        copy.start()
+        sends.append(copy)
+
+    def cut_of(p, r):
+        start, size = cuts[r]
+        return pl.ds(pl.multiple_of(p * rows + start, 16), size)
+
+    def send_queries(r):
+        start, size = cuts[r]
+        for h in range(share):
+            for p in peers:
+                launch(
+                    to_seq(
+                        vq.at[pl.ds(start, size), head_cols(p, h)],
+                        qkv.at[2, h, cut_of(me, r)],
+                        q_send.at[r, h, p],
+                        q_recv.at[r, h, me],
+                        p,
+                    )
+                )
+
+    for h in range(share):
+        for kind, ref in enumerate((vk, vv)):
+            for p in peers:
+                launch(
+                    to_seq(
+                        ref.at[:, head_cols(p, h)],
+                        qkv.at[kind, h, my_rows],
+                        kv_send.at[kind, h, p],
+                        kv_recv.at[kind, h, me],
+                        p,
+                    )
+                )
+    send_queries(0)
+    for kind, ref in enumerate((ak, av, aq)):
+        for p in peers:
+            launch(to_seq(ref, audio.at[kind, my_audio], audio_send.at[kind, p], audio_recv.at[kind, me], p))
+    for r in range(1, len(cuts)):
+        send_queries(r)
+
+    weight_copy = pltpu.make_async_copy(weight, weight_v, weight_sem)
+    weight_copy.start()
+
+    def wait_from(src, dst, send_sem, recv_sem, p):
+        to_seq(src, dst, send_sem, recv_sem, p).wait_recv()
 
     def rows_of(p):
         return pl.ds(pl.multiple_of(p * rows, rows), rows)
@@ -288,36 +298,49 @@
     def audio_rows_of(p):
         return pl.ds(pl.multiple_of(p * audio_rows, audio_rows), audio_rows)
 
-    def attend_head(h):
-        for kind in range(3):
-            local_copies[h * 3 + kind].wait()
-        for kind in range(3):
-            for p in peers:
-                wait_from(
-                    vk.at[:, head_cols(p, h)],
-                    qkv.at[kind, h, rows_of(p)],
-                    qkv_send.at[kind, h, p],
-                    qkv_recv.at[kind, h, p],
-                    p,
-                )
-        keyset, values = qkv[0, h], qkv[1, h]
-        for p in peers + [me]:
-            _, row_sum, numerator = softmax_parts(qkv[2, h, rows_of(p)], keyset, values)
-            result = (numerator / row_sum).astype(jnp.bfloat16)
-            if p is me:
-                gathered[h, me] = result
-            else:
-                heads_out[h, p] = result
-                copy = pltpu.make_async_remote_copy(
-                    src_ref=heads_out.at[h, p],
-                    dst_ref=gathered.at[h, me],
-                    send_sem=out_send.at[h, p],
-                    recv_sem=out_recv.at[h, me],
-                    device_id={"seq": p},
-                    device_id_type=MESH,
-                )
-                copy.start()
-                sends.append(copy)
+    def wait_keys():
+        for copy in local_copies:
+            copy.wait()
+        for h in range(share):
+            for kind, ref in enumerate((vk, vv)):
+                for p in peers:
+                    wait_from(
+                        ref.at[:, head_cols(p, h)],
+                        qkv.at[kind, h, rows_of(p)],
+                        kv_send.at[kind, h, p],
+                        kv_recv.at[kind, h, p],
+                        p,
+                    )
+
+    def attend_rows(r):
+        start, size = cuts[r]
+        here = pl.ds(start, size)
+        for h in range(share):
+            keyset, values = qkv[0, h], qkv[1, h]
+            for p in peers + [me]:
+                if p is not me:
+                    wait_from(
+                        vq.at[here, head_cols(p, h)],
+                        qkv.at[2, h, cut_of(p, r)],
+                        q_send.at[r, h, p],
+                        q_recv.at[r, h, p],
+                        p,
+                    )
+                _, row_sum, numerator = softmax_parts(qkv[2, h, cut_of(p, r)], keyset, values)
+                result = (numerator / row_sum).astype(jnp.bfloat16)
+                if p is me:
+                    gathered[h, me, here] = result
+                else:
+                    heads_out[h, p, here] = result
+                    launch(
+                        to_seq(
+                            heads_out.at[h, p, here],
+                            gathered.at[h, me, here],
+                            out_send.at[r, h, p],
+                            out_recv.at[r, h, me],
+                            p,
+                        )
+                    )
 
     def cross_parts():
         for i in range(3):
@@ -377,97 +400,104 @@
             numerator = sum(f * n.astype(jnp.float32) for f, n in zip(factors, parts))
             across_ref[:, cols] = (numerator / row_sum).astype(jnp.bfloat16)
 
-    def wait_heads(h):
-        for p in peers:
-            wait_from(heads_out.at[h, p], gathered.at[h, p], out_send.at[h, p], out_recv.at[h, p], p)
-        for p in range(seq):
-            weight_copies[h * seq + p].wait()
-        return jnp.concatenate([gathered[h, p] for p in range(seq)], axis=1)
-
-    def product(attended, h, target, j):
+    def wait_heads(r):
+        here = pl.ds(*cuts[r])
+        for h in range(share):
+            for p in peers:
+                wait_from(
+                    heads_out.at[h, p, here],
+                    gathered.at[h, p, here],
+                    out_send.at[r, h, p],
+                    out_recv.at[r, h, p],
+                    p,
+                )
+        return jnp.concatenate(
+            [gathered[h, p, here] for p in range(seq) for h in range(share)], axis=1
+        )
+
+    def product(attended, d, side, j):
+        target = far_chips[d] * 2 + (core if side else 1 - core)
         cols = pl.ds(pl.multiple_of(target * width + j * WIDE, WIDE), WIDE)
-        return jnp.dot(attended, weight_v[h, :, cols], preferred_element_type=jnp.float32)
-
-    attend_head(0)
-    cross_parts()
-    for h in range(1, share):
-        attend_head(h)
-    cross_finish()
-    loads[3].wait()
-
-    slots = [(d, side) for d in list(range(1, chips)) + [0] for side in range(2)]
-
-    def owner_of(d, side):
-        return far_chips[d] * 2 + (core if side else 1 - core)
-
-    for h in range(share - 1):
-        attended = wait_heads(h)
-        for d, side in slots:
-            for j in range(pieces):
-                value = product(attended, h, owner_of(d, side), j)
-                if h:
-                    value = value + total[d, side, j]
-                total[d, side, j] = value
-    last = share - 1
-    attended = wait_heads(last)
-
-    def final(d, side, j):
-        value = product(attended, last, owner_of(d, side), j)
-        if last:
-            value = value + total[d, side, j]
-        return value
-
-    def pair_copy(d, j):
+        return jnp.dot(attended, weight_v[:, cols], preferred_element_type=jnp.float32)
+
+    def pair_copy(r, d, j):
+        here = pl.ds(*cuts[r])
         return pltpu.make_async_remote_copy(
-            src_ref=pair_out.at[d, j],
-            dst_ref=pair_in.at[d, j],
-            send_sem=pair_send.at[d, j],
-            recv_sem=pair_recv.at[d, j],
+            src_ref=pair_out.at[d, j, here],
+            dst_ref=pair_in.at[d, j, here],
+            send_sem=pair_send.at[r, d, j],
+            recv_sem=pair_recv.at[r, d, j],
             device_id={"tensor": sibling},
             device_id_type=MESH,
         )
 
-    def far_copy(d, j):
+    def far_copy(r, d, j):
+        here = pl.ds(*cuts[r])
         return pltpu.make_async_remote_copy(
-            src_ref=far_out.at[d - 1, j],
-            dst_ref=far_in.at[d - 1, j],
-            send_sem=far_send.at[d - 1, j],
-            recv_sem=far_recv.at[d - 1, j],
+            src_ref=far_out.at[d - 1, j, here],
+            dst_ref=far_in.at[d - 1, j, here],
+            send_sem=far_send.at[r, d - 1, j],
+            recv_sem=far_recv.at[r, d - 1, j],
             device_id={"tensor": far_chips[d] * 2 + core},
             device_id_type=MESH,
         )
 
-    def send_pair(d, j):
-        pair_out[d, j] = final(d, 0, j).astype(jnp.bfloat16)
-        copy = pair_copy(d, j)
-        copy.start()
-        sends.append(copy)
-
-    def send_far(d, j, value):
-        pair_copy(d, j).wait_recv()
-        far_out[d - 1, j] = (value + pair_in[d, j].astype(jnp.float32)).astype(jnp.bfloat16)
-        copy = far_copy(d, j)
-        copy.start()
-        sends.append(copy)
-
-    steps = [(d, j) for d in range(1, chips) for j in range(pieces)]
-    for d, j in steps:
-        send_pair(d, j)
-    for d, j in steps:
-        send_far(d, j, final(d, 1, j))
-    for j in range(pieces):
-        send_pair(0, j)
-    for j in range(pieces):
-        total[0, 1, j] = final(0, 1, j) + stream_v[:, j * WIDE : (j + 1) * WIDE].astype(jnp.float32)
-    for j in range(pieces):
-        pair_copy(0, j).wait_recv()
-        value = total[0, 1, j] + pair_in[0, j].astype(jnp.float32)
-        for d in range(1, chips):
-            far_copy(d, j).wait_recv()
-            value = value + far_in[d - 1, j].astype(jnp.float32)
-        next_ref[:, j * WIDE : (j + 1) * WIDE] = value.astype(jnp.bfloat16)
+    def share_rows(r):
+        here = pl.ds(*cuts[r])
+        attended = wait_heads(r)
+        if r == 0:
+            weight_copy.wait()
+        steps = [(d, j) for d in range(1, chips) for j in range(pieces)]
+        for d, j in steps + [(0, j) for j in range(pieces)]:
+            pair_out[d, j, here] = product(attended, d, 0, j).astype(jnp.bfloat16)
+            launch(pair_copy(r, d, j))
+            if d:
+                mine = product(attended, d, 1, j)
+                pair_copy(r, d, j).wait_recv()
+                far_out[d - 1, j, here] = (mine + pair_in[d, j, here].astype(jnp.float32)).astype(
+                    jnp.bfloat16
+                )
+                launch(far_copy(r, d, j))
+        for j in range(pieces):
+            block = slice(j * WIDE, (j + 1) * WIDE)
+            kept[here, block] = product(attended, 0, 1, j) + stream_v[here, block].astype(jnp.float32)
+
+    def close_rows(r):
+        here = pl.ds(*cuts[r])
+        for j in range(pieces):
+            block = slice(j * WIDE, (j + 1) * WIDE)
+            pair_copy(r, 0, j).wait_recv()
+            value = kept[here, block] + pair_in[0, j, here].astype(jnp.float32)
+            for d in range(1, chips):
+                far_copy(r, d, j).wait_recv()
+                value = value + far_in[d - 1, j, here].astype(jnp.float32)
+            next_ref[here, block] = value.astype(jnp.bfloat16)
+
+    wait_keys()
+    attend_rows(0)
+    cross_parts()
+    for r in range(1, len(cuts)):
+        attend_rows(r)
+    loads[3].wait()
+    for r in range(len(cuts)):
+        share_rows(r)
+        if r == 0:
+            cross_finish()
+    for r in range(len(cuts)):
+        close_rows(r)
     for copy in sends:
         copy.wait_send()
+
+
+def row_cuts(rows):
+    first = max(rows * FIRST // 4 // 16 * 16, 16)
+    return [(0, first), (first, rows - first)] if first < rows else [(0, rows)]
+
+
+def write_out(*refs):
+    half = len(refs) // 2
+    for src, dst in zip(refs[:half], refs[half:]):
+        dst[...] = src[...]
 
 
 def fused(seq, tensor, *operands):
@@ -478,16 +508,15 @@
     chips = tensor // 2
     width = weight.shape[1] // tensor
     pieces = width // WIDE
+    groups = len(row_cuts(rows))
     bf16, f32, dma = jnp.bfloat16, jnp.float32, pltpu.SemaphoreType.DMA
-    return pl.pallas_call(
+    shapes = tuple(jax.ShapeDtypeStruct(x.shape, bf16) for x in (vs, cq, aq))
+    whole = pl.BlockSpec(memory_space=pltpu.VMEM)
+    results = pl.pallas_call(
         functools.partial(block_kernel, seq, tensor),
-        out_shape=(
-            jax.ShapeDtypeStruct(vs.shape, bf16),
-            jax.ShapeDtypeStruct(cq.shape, bf16),
-            jax.ShapeDtypeStruct(aq.shape, bf16),
-        ),
-        in_specs=[pl.BlockSpec(memory_space=pl.ANY)] * 11,
-        out_specs=tuple([pl.BlockSpec(memory_space=pltpu.VMEM)] * 3),
+        out_shape=tuple(pltpu.VMEM(x.shape, bf16) for x in (vs, cq, aq)),
+        in_specs=[pl.BlockSpec(memory_space=pltpu.HBM)] * 11,
+        out_specs=(whole,) * 3,
         scratch_shapes=[
             pltpu.VMEM((3, share, seq * rows, HD), bf16),
             pltpu.VMEM((share, seq, rows, HD), bf16),
@@ -501,17 +530,19 @@
             pltpu.VMEM(ck.shape, bf16),
             pltpu.VMEM(cv.shape, bf16),
             pltpu.VMEM(vs.shape, bf16),
-            pltpu.VMEM((share, seq * HD, weight.shape[1]), bf16),
-            pltpu.VMEM((chips, 2, pieces, rows, WIDE), f32),
+            pltpu.VMEM(weight.shape, bf16),
+            pltpu.VMEM(vs.shape, f32),
             pltpu.VMEM((chips, pieces, rows, WIDE), bf16),
             pltpu.VMEM((chips, pieces, rows, WIDE), bf16),
             pltpu.VMEM((max(chips - 1, 1), pieces, rows, WIDE), bf16),
             pltpu.VMEM((max(chips - 1, 1), pieces, rows, WIDE), bf16),
-            dma((3, share, seq)),
-            dma((3, share, seq)),
+            dma((2, share, seq)),
+            dma((2, share, seq)),
+            dma((groups, share, seq)),
+            dma((groups, share, seq)),
             dma((3, share)),
-            dma((share, seq)),
-            dma((share, seq)),
+            dma((groups, share, seq)),
+            dma((groups, share, seq)),
             dma((3, seq)),
             dma((3, seq)),
             dma((3,)),
@@ -520,16 +551,23 @@
             dma((seq,)),
             dma((seq,)),
             dma((4,)),
-            dma((share, seq)),
-            dma((chips, pieces)),
-            dma((chips, pieces)),
-            dma((max(chips - 1, 1), pieces)),
-            dma((max(chips - 1, 1), pieces)),
+            dma(()),
+            dma((groups, chips, pieces)),
+            dma((groups, chips, pieces)),
+            dma((groups, max(chips - 1, 1), pieces)),
+            dma((groups, max(chips - 1, 1), pieces)),
         ],
         compiler_params=pltpu.CompilerParams(
             collective_id=0, has_side_effects=True, vmem_limit_bytes=60000000
         ),
     )(*operands)
+    return pl.pallas_call(
+        write_out,
+        out_shape=shapes,
+        in_specs=[whole] * 3,
+        out_specs=(whole,) * 3,
+        compiler_params=pltpu.CompilerParams(vmem_limit_bytes=8 * 2**20),
+    )(*results)
 
 
 def fits(mesh, operands):
@@ -543,8 +581,8 @@
         and aq.shape[0] % 16 == 0
         and vq.shape[0] % 16 == 0
         and 2 * (cq.shape[1] // HD) <= HD
-        and weight.size * 2 <= 16 * 2**20
-        and vq.shape[0] <= 256
+        and weight.size * 2 <= 10 * 2**20
+        and vq.shape[0] <= 128
         and seq <= 8
     )
 

time: 52.8 us -> 52.7 us (level)
  Pallas kernels: 47.3 us -> 51.9 us
  local copies, waits for them, and re-layouts: 4.56 us -> 0 us
    pallas_call x1 -> x2, Pallas kernels: 47.3 us -> 51.9 us  [the longest x1 51.1 us: fused(): pl.pallas_call(functools.partial(block_kernel, seq, tensor), out_shape=tu...]
    unnamed x3 -> x0, local copies, waits for them, and re-layouts: 4.56 us -> none
where the time goes in v2:
time: 52.7 us; the launch traced here: 52.5 us
  Pallas kernels  51.9 us (98%)
  between operations  0.64 us (1%)
    pallas_call x1, Pallas kernels, fused(): pl.pallas_call(functools.partial(block_kernel, seq, tensor), out_shape=tu...  51.1 us

profile of v2, /device:TPU:0, one launch (start us, length us, event | category | flops | bytes accessed | tf_op | source)
XLA Modules:
  0.0 52.5 jit_solution(3547034264752225328)
XLA Ops:
  0.6 51.1 %shard_map.130 = (bf16[128,1024]{1,0:T(8,128)(2,1)S(1)}, bf16[128,512]{1,0:T(8,128)(2,1)S(1)}, bf16[16,512]{1,0:T(8,128)(2,1)S(1)}) custom-call(bf16[128,1024]{1,0:T(8,128)(2,1)} %vq.1, bf16[128,1024]{1,0:T(8,128)(2,1)} %vk.1, bf16[128,1024]{1,0:T(8,128)(2,1)} %vv.1, bf16[128,1024]{1,0:T(8,128)(2,1)} %vs.1, bf16[1024,4096]{1,0:T(8,128)(2,1)} %weight.1, ...), custom_call_target="tpu_custom_call" | custom-call | tf_op jit(solution)/shard_map/pallas_call | solution.py:515
  51.8 0.8 %shard_map.131 = (bf16[128,1024]{1,0:T(8,128)(2,1)}, bf16[128,512]{1,0:T(8,128)(2,1)}, bf16[16,512]{1,0:T(8,128)(2,1)}) custom-call(bf16[128,1024]{1,0:T(8,128)(2,1)S(1)} %get-tuple-element.6.refs_0_, bf16[128,512]{1,0:T(8,128)(2,1)S(1)} %get-tuple-element.7.refs_1_, bf16[16,512]{1,0:T(8,128)(2,1)S(1)} %get-tuple-element.8.refs_2_), custom_call_target="tpu_custom_call" | custom-call | tf_op jit(solution)/shard_map/pallas_call | solution.py:564

commit v3 on v2

--- a/solution.py
+++ b/solution.py
@@ -111,7 +111,7 @@
 
 MESH = pl.DeviceIdType.MESH
 NT = (((1,), (1,)), ((), ()))
-WIDE = 256
+WIDE = 512
 FIRST = 3
 
 
@@ -267,6 +267,50 @@
                     )
                 )
 
+    def rows_of(p):
+        return pl.ds(pl.multiple_of(p * rows, rows), rows)
+
+    def audio_rows_of(p):
+        return pl.ds(pl.multiple_of(p * audio_rows, audio_rows), audio_rows)
+
+    def audio_hop(step, way):
+        shard = lax.rem(me - way * step + seq, seq)
+        here = audio_rows_of(shard)
+        return to_seq(
+            audio.at[:, here],
+            audio.at[:, here],
+            audio_send.at[step, (way + 1) // 2],
+            audio_recv.at[shard],
+            lax.rem(me + way + seq, seq),
+        )
+
+    def on_line(step, way):
+        source, target = me - way * step, me + way
+        return (source >= 0) & (source < seq) & (target >= 0) & (target < seq)
+
+    def pass_audio(step):
+        for way in (1, -1):
+
+            @pl.when(on_line(step, way))
+            def _():
+                copy = audio_hop(step, way)
+                if step:
+                    copy.wait_recv()
+                copy.start()
+
+    def end_audio():
+        for step in range(1, seq):
+            for way in (1, -1):
+                source, target = me - way * step, me + way
+                last = (target < 0) | (target >= seq)
+
+                @pl.when((source >= 0) & (source < seq) & last)
+                def _():
+                    audio_hop(step, way).wait_recv()
+
+    for copy in audio_copies:
+        copy.wait()
+    pass_audio(0)
     for h in range(share):
         for kind, ref in enumerate((vk, vv)):
             for p in peers:
@@ -279,10 +323,8 @@
                         p,
                     )
                 )
+    pass_audio(1)
     send_queries(0)
-    for kind, ref in enumerate((ak, av, aq)):
-        for p in peers:
-            launch(to_seq(ref, audio.at[kind, my_audio], audio_send.at[kind, p], audio_recv.at[kind, me], p))
     for r in range(1, len(cuts)):
         send_queries(r)
 
@@ -291,12 +333,6 @@
 
     def wait_from(src, dst, send_sem, recv_sem, p):
         to_seq(src, dst, send_sem, recv_sem, p).wait_recv()
-
-    def rows_of(p):
-        return pl.ds(pl.multiple_of(p * rows, rows), rows)
-
-    def audio_rows_of(p):
-        return pl.ds(pl.multiple_of(p * audio_rows, audio_rows), audio_rows)
 
     def wait_keys():
         for copy in local_copies:
@@ -345,16 +381,7 @@
     def cross_parts():
         for i in range(3):
             loads[i].wait()
-        for kind in range(3):
-            audio_copies[kind].wait()
-            for p in peers:
-                wait_from(
-                    ak,
-                    audio.at[kind, audio_rows_of(p)],
-                    audio_send.at[kind, p],
-                    audio_recv.at[kind, p],
-                    p,
-                )
+        end_audio()
         lane = lax.broadcasted_iota(jnp.int32, (seq * audio_rows, HD), 1)
         held = jnp.zeros((seq * audio_rows, HD), jnp.float32)
         for c in range(cross_heads):
@@ -448,16 +475,19 @@
         if r == 0:
             weight_copy.wait()
         steps = [(d, j) for d in range(1, chips) for j in range(pieces)]
-        for d, j in steps + [(0, j) for j in range(pieces)]:
+        for d, j in steps:
             pair_out[d, j, here] = product(attended, d, 0, j).astype(jnp.bfloat16)
             launch(pair_copy(r, d, j))
-            if d:
-                mine = product(attended, d, 1, j)
-                pair_copy(r, d, j).wait_recv()
-                far_out[d - 1, j, here] = (mine + pair_in[d, j, here].astype(jnp.float32)).astype(
-                    jnp.bfloat16
-                )
-                launch(far_copy(r, d, j))
+        for d, j in steps:
+            mine = product(attended, d, 1, j)
+            pair_copy(r, d, j).wait_recv()
+            far_out[d - 1, j, here] = (mine + pair_in[d, j, here].astype(jnp.float32)).astype(
+                jnp.bfloat16
+            )
+            launch(far_copy(r, d, j))
+        for j in range(pieces):
+            pair_out[0, j, here] = product(attended, 0, 0, j).astype(jnp.bfloat16)
+            launch(pair_copy(r, 0, j))
         for j in range(pieces):
             block = slice(j * WIDE, (j + 1) * WIDE)
             kept[here, block] = product(attended, 0, 1, j) + stream_v[here, block].astype(jnp.float32)
@@ -474,6 +504,8 @@
             next_ref[here, block] = value.astype(jnp.bfloat16)
 
     wait_keys()
+    for step in range(2, seq - 1):
+        pass_audio(step)
     attend_rows(0)
     cross_parts()
     for r in range(1, len(cuts)):
@@ -487,6 +519,12 @@
         close_rows(r)
     for copy in sends:
         copy.wait_send()
+    for step in range(seq - 1):
+        for way in (1, -1):
+
+            @pl.when(on_line(step, way))
+            def _():
+                audio_hop(step, way).wait_send()
 
 
 def row_cuts(rows):
@@ -543,8 +581,8 @@
             dma((3, share)),
             dma((groups, share, seq)),
             dma((groups, share, seq)),
-            dma((3, seq)),
-            dma((3, seq)),
+            dma((seq, 2)),
+            dma((seq,)),
             dma((3,)),
             dma((seq,)),
             dma((seq,)),

time: 52.7 us -> 44 us (0.83)
  Pallas kernels: 51.9 us -> 43.2 us
    pallas_call x1, Pallas kernels: 51.1 us -> 42.4 us  [fused(): pl.pallas_call(functools.partial(block_kernel, seq, tensor), out_shape=tu...]
where the time goes in v3:
time: 44 us; the launch traced here: 43.9 us
  Pallas kernels  43.2 us (98%)
  between operations  0.64 us (1%)
    pallas_call x1, Pallas kernels, fused(): pl.pallas_call(functools.partial(block_kernel, seq, tensor), out_shape=tu...  42.4 us

profile of v3, /device:TPU:0, one launch (start us, length us, event | category | flops | bytes accessed | tf_op | source)
XLA Modules:
  0.0 43.9 jit_solution(15067371003769772888)
XLA Ops:
  0.6 42.4 %shard_map.130 = (bf16[128,1024]{1,0:T(8,128)(2,1)S(1)}, bf16[128,512]{1,0:T(8,128)(2,1)S(1)}, bf16[16,512]{1,0:T(8,128)(2,1)S(1)}) custom-call(bf16[128,1024]{1,0:T(8,128)(2,1)} %vq.1, bf16[128,1024]{1,0:T(8,128)(2,1)} %vk.1, bf16[128,1024]{1,0:T(8,128)(2,1)} %vv.1, bf16[128,1024]{1,0:T(8,128)(2,1)} %vs.1, bf16[1024,4096]{1,0:T(8,128)(2,1)} %weight.1, ...), custom_call_target="tpu_custom_call" | custom-call | tf_op jit(solution)/shard_map/pallas_call | solution.py:553
  43.1 0.8 %shard_map.131 = (bf16[128,1024]{1,0:T(8,128)(2,1)}, bf16[128,512]{1,0:T(8,128)(2,1)}, bf16[16,512]{1,0:T(8,128)(2,1)}) custom-call(bf16[128,1024]{1,0:T(8,128)(2,1)S(1)} %get-tuple-element.6.refs_0_, bf16[128,512]{1,0:T(8,128)(2,1)S(1)} %get-tuple-element.7.refs_1_, bf16[16,512]{1,0:T(8,128)(2,1)S(1)} %get-tuple-element.8.refs_2_), custom_call_target="tpu_custom_call" | custom-call | tf_op jit(solution)/shard_map/pallas_call | solution.py:602

commit v4 on v3

--- a/solution.py
+++ b/solution.py
@@ -112,7 +112,7 @@
 MESH = pl.DeviceIdType.MESH
 NT = (((1,), (1,)), ((), ()))
 WIDE = 512
-FIRST = 3
+FIRST = 4
 
 
 def softmax_parts(queries, keyset, values):
@@ -506,15 +506,13 @@
     wait_keys()
     for step in range(2, seq - 1):
         pass_audio(step)
-    attend_rows(0)
+    for r in range(len(cuts)):
+        attend_rows(r)
     cross_parts()
-    for r in range(1, len(cuts)):
-        attend_rows(r)
     loads[3].wait()
     for r in range(len(cuts)):
         share_rows(r)
-        if r == 0:
-            cross_finish()
+    cross_finish()
     for r in range(len(cuts)):
         close_rows(r)
     for copy in sends:

time: 44 us -> 43.6 us (level)
    pallas_call x1, Pallas kernels: 42.4 us -> 42 us  [fused(): pl.pallas_call(functools.partial(block_kernel, seq, tensor), out_shape=tu...]
where the time goes in v4:
time: 43.6 us; the launch traced here: 43.4 us
  Pallas kernels  42.8 us (98%)
  between operations  0.64 us (1%)
    pallas_call x1, Pallas kernels, fused(): pl.pallas_call(functools.partial(block_kernel, seq, tensor), out_shape=tu...  42 us

profile of v4, /device:TPU:0, one launch (start us, length us, event | category | flops | bytes accessed | tf_op | source)
XLA Modules:
  0.0 43.4 jit_solution(14397748378109471345)
XLA Ops:
  0.6 42.0 %shard_map.130 = (bf16[128,1024]{1,0:T(8,128)(2,1)S(1)}, bf16[128,512]{1,0:T(8,128)(2,1)S(1)}, bf16[16,512]{1,0:T(8,128)(2,1)S(1)}) custom-call(bf16[128,1024]{1,0:T(8,128)(2,1)} %vq.1, bf16[128,1024]{1,0:T(8,128)(2,1)} %vk.1, bf16[128,1024]{1,0:T(8,128)(2,1)} %vv.1, bf16[128,1024]{1,0:T(8,128)(2,1)} %vs.1, bf16[1024,4096]{1,0:T(8,128)(2,1)} %weight.1, ...), custom_call_target="tpu_custom_call" | custom-call | tf_op jit(solution)/shard_map/pallas_call | solution.py:551
  42.6 0.8 %shard_map.131 = (bf16[128,1024]{1,0:T(8,128)(2,1)}, bf16[128,512]{1,0:T(8,128)(2,1)}, bf16[16,512]{1,0:T(8,128)(2,1)}) custom-call(bf16[128,1024]{1,0:T(8,128)(2,1)S(1)} %get-tuple-element.6.refs_0_, bf16[128,512]{1,0:T(8,128)(2,1)S(1)} %get-tuple-element.7.refs_1_, bf16[16,512]{1,0:T(8,128)(2,1)S(1)} %get-tuple-element.8.refs_2_), custom_call_target="tpu_custom_call" | custom-call | tf_op jit(solution)/shard_map/pallas_call | solution.py:600
